TPU v7x, 256 devices: a whole 4x4x8 slice. The times are simulated.
256 devices in a mesh: row: 32 (over z_lo, x, core), col: 8 (over z_hi, y).
Axes of the slice: x: 4, y: 4, z: 8 (z_hi: 2, z_lo: 4; z = z_hi * 4 + z_lo), core: 2. Of those that a mesh axis runs over, the one named last changes fastest.
Arguments:
- positions: float32 [3, 1048576], P(None, ('row', 'col')), may hold values from 0 to 385, as said below
- atom_type: int32 [1048576], P(('row', 'col')), may hold values from 0 to 5
- krylov: float32 [16, 1048576], P(None, ('row', 'col')), may hold values from -6 to 6
- block_order: int32 [1048576], P(('row', 'col')), may hold values from 0 to 4095, as said below
- type_width: float32 [6], replicated, may hold values from 0.5 to 2.5
- type_hard: float32 [6], replicated, may hold values from 1 to 4
- pair_rows: int32 [32, 8, 512], P('row', 'col'), may hold values from 0 to 255, as said below
- pair_cols: int32 [32, 8, 512], P('row', 'col'), may hold values from 0 to 1023, as said below
- pair_count: int32 [32, 8], P('row', 'col'), may hold values from 1 to 512, as said below
Outputs:
- coulomb_response: float32 [16, 1048576], P(None, ('row', 'col'))
Inputs may be any that keep to these rules, and one draw needn't show every extreme that they name: `positions`: global block g is a cell of a grid with coordinates (g // 256, (g // 32) % 8, g % 32); each atom of block g lies in the box of sides 44, 30 and 44 whose lowest corner is the cell's coordinates times 11, 5 and 11. `block_order`: within each device's shard of 4096 atoms, the entries are a permutation of 0 to 4095. `pair_rows`: in slots below pair_count the pairs (i, j) are distinct, have i <= j, and their grid cells differ by at most 2 along the first and third dimensions and at most 4 along the second; for device (r, c), pair_cols // 32 is r, r + 1 or r + 2 there. Other slots hold indices in range that are not used. `pair_cols`: see pair_rows. `pair_count`: some device's list is full.
All inputs are finite; a program needn't handle non-finite values.
Results may differ from a plain program's by a relative error of at most 0.00665.
Values may be sent and summed in bfloat16 or wider, within the bound.
No kernel may reach another device: no remote copies, remote signals or barrier semaphores. Data moves between devices by JAX's collectives and lax.ppermute only.
A program may use at most 128 MiB of HBM per device.

v0:
```python
import functools

import jax
import jax.numpy as jnp
import ml_dtypes
import numpy as np
from jax import lax
from jax.experimental import pallas as pl
from jax.experimental.pallas import tpu as pltpu
from jax.sharding import PartitionSpec as P

BLK = 128
VECS = 16
NTYPES = 6
BLOCKS = 32
HALF = 4 * BLOCKS
COLS = 3 * BLOCKS
ROWS = VECS + 8
DEPTH = 80
UNROLL = 8
SLOTS = 512
SLOT_SPAN = SLOTS + BLK
SPARE = 3 << 22
PREP_BLOCKS = 8
CELL = (11.0, 5.0, 11.0)
BOX = (44.0, 30.0, 44.0)
SOFTENING = 0.5

ERF_COEFFS = (
    1.2732353673862733,
    0.23198340332298037,
    0.01001461653081914,
    -0.0013852189685132543,
    7.466663090475016e-05,
)


def time_cost(microseconds):
    return pl.CostEstimate(
        flops=int(microseconds * 1_000_000_000), transcendentals=0, bytes_accessed=1_000_000
    )


PAIR_COST = time_cost(16)

VMEM = pl.BlockSpec(memory_space=pltpu.VMEM)
SMEM = pl.BlockSpec(memory_space=pltpu.SMEM)
ANY = pl.BlockSpec(memory_space=pl.ANY)
Y_GROUPS = [[0, 1, 2, 3], [4, 5, 6, 7]]
F32 = jnp.float32
BF16 = jnp.bfloat16


def sublane():
    return lax.broadcasted_iota(jnp.int32, (8, BLK), 0)


def split3(value):
    high = value.astype(BF16).astype(F32)
    rest = value - high
    middle = rest.astype(BF16).astype(F32)
    return high, middle, rest - middle


def lane_gather(source, index):
    return jnp.take_along_axis(source, index, axis=1, mode="promise_in_bounds")


def here():
    return lax.axis_index("row"), lax.axis_index("col")


def prep_kernel(
    positions_hbm, type_hbm, krylov_hbm, order_hbm, packed, geometry, positions, atom_type, krylov, order, done
):
    loads = [
        pltpu.make_async_copy(source, target, done.at[k])
        for k, (source, target) in enumerate(
            (
                (krylov_hbm, krylov),
                (positions_hbm, positions),
                (type_hbm, atom_type),
                (order_hbm, order),
            )
        )
    ]
    for load in loads:
        load.start()
    place = here()
    for load in loads[1:]:
        load.wait()
    middle = BLOCKS // 2 * BLK
    geometry[0:3, :] = positions[:, 0:middle]
    geometry[3:4, :] = atom_type[:, 0:middle].astype(F32)
    geometry[4:7, :] = positions[:, middle:]
    geometry[7:8, :] = atom_type[:, middle:].astype(F32)
    level = sublane()
    corner_x = CELL[0] * place[0].astype(F32) + BOX[0] / 2
    corner_y = CELL[1] * place[1].astype(F32) + BOX[1] / 2

    def one_block(block):
        wanted = jnp.broadcast_to(order[pl.ds(block, 1), :], (8, BLK))
        chunk = wanted >> 7
        lane = wanted & 127
        folded = chunk & (BLOCKS // 2 - 1)
        top = jnp.zeros((8, BLK), F32)
        low = jnp.zeros((8, BLK), F32)
        geo = jnp.zeros((8, BLK), F32)
        for s in range(BLOCKS):
            span = slice(s * BLK, (s + 1) * BLK)
            top = jnp.where(chunk == s, lane_gather(krylov[0:8, span], lane), top)
            low = jnp.where(chunk == s, lane_gather(krylov[8:16, span], lane), low)
            if s < BLOCKS // 2:
                geo = jnp.where(folded == s, lane_gather(geometry[:, span], lane), geo)
        geo = jnp.where(chunk < BLOCKS // 2, geo, pltpu.roll(geo, 4, 0))
        corner_z = CELL[2] * block.astype(F32) + BOX[2] / 2
        corner = jnp.where(
            level == 0, corner_x, jnp.where(level == 1, corner_y, jnp.where(level == 2, corner_z, 0.0))
        )
        local = jnp.where(level < 4, geo - corner, 0.0)
        coarse = jnp.floor(local * 4.0 + 0.5) * 0.25
        fine = jnp.where(level < 3, local - coarse, local)
        coded = jnp.where(level < 3, coarse, pltpu.roll(fine, 3, 0))
        packed[block, 0:VECS, :] = jnp.concatenate([top, low], axis=0).astype(BF16)
        packed[block, VECS:ROWS, :] = coded.astype(BF16)

    def some_blocks(turn, carry):
        for extra in range(PREP_BLOCKS):
            one_block(turn * PREP_BLOCKS + extra)
        return carry

    loads[0].wait()
    lax.fori_loop(0, BLOCKS // PREP_BLOCKS, some_blocks, 0)


def side_kernel(
    count_hbm, rows_hbm, cols_hbm, order_hbm, inverse, codes, counts, count, rows, cols, order, done
):
    loads = [
        pltpu.make_async_copy(source, target, done.at[k])
        for k, (source, target) in enumerate(
            ((count_hbm, count), (rows_hbm, rows), (cols_hbm, cols), (order_hbm, order))
        )
    ]
    for load in loads:
        load.start()
    place = here()
    for load in loads:
        load.wait()
    row = rows[...]
    col = cols[...] - place[0] * BLOCKS
    step_y = place[1] - (row >> 5) + 4
    step_z = (col & 31) - (row & 31) + 2
    step = ((col >> 5) * 9 + step_y) * 5 + step_z
    diagonal = jnp.logical_and(col < BLOCKS, row == place[1] * BLOCKS + col)
    code = (row & 127) | (col << 7) | (step << 14) | (diagonal.astype(jnp.int32) << 22)
    live = lax.broadcasted_iota(jnp.int32, (1, SLOTS), 1) < count[0, 0]
    same = (row >> 7) == (place[1] >> 2)
    near = jnp.logical_and(live, same).astype(F32)
    far = jnp.logical_and(live, jnp.logical_not(same)).astype(F32)
    level = lax.broadcasted_iota(jnp.int32, (8, SLOTS), 0)
    wide = lambda v: jnp.broadcast_to(v, (8, SLOTS))
    flags = jnp.where(level == 0, wide(near), jnp.where(level == 1, wide(far), 0.0)).astype(BF16)
    earlier = (
        (lax.broadcasted_iota(jnp.int32, (SLOTS, SLOTS), 0) < lax.broadcasted_iota(jnp.int32, (SLOTS, SLOTS), 1))
        .astype(F32)
        .astype(BF16)
    )
    ranks = jnp.dot(flags, earlier, preferred_element_type=F32)
    target = jnp.where(
        near > 0.5, ranks[0:1], jnp.where(far > 0.5, ranks[1:2] + float(SLOT_SPAN), -1.0)
    ).astype(jnp.int32)
    chosen = (
        (
            lax.broadcasted_iota(jnp.int32, (2 * SLOT_SPAN, SLOTS), 0)
            == jnp.broadcast_to(target, (2 * SLOT_SPAN, SLOTS))
        )
        .astype(F32)
        .astype(BF16)
    )
    low = wide((code & 255).astype(F32))
    middle = wide(((code >> 8) & 255).astype(F32))
    high = wide((code >> 16).astype(F32))
    parts = jnp.where(level == 0, low, jnp.where(level == 1, middle, jnp.where(level == 2, high, 0.0)))
    moved = lax.dot_general(
        parts.astype(BF16), chosen, (((1,), (1,)), ((), ())), preferred_element_type=F32
    )
    listed = (moved[0:1] + moved[1:2] * 256.0 + moved[2:3] * 65536.0).astype(jnp.int32)
    near_count = jnp.sum(near).astype(jnp.int32)
    far_count = jnp.sum(far).astype(jnp.int32)
    spot = lax.broadcasted_iota(jnp.int32, (1, 2 * SLOT_SPAN), 1)
    in_near = spot < SLOT_SPAN
    used = jnp.where(in_near, spot, spot - SLOT_SPAN) < jnp.where(in_near, near_count, far_count)
    codes[...] = jnp.where(used, listed, SPARE)
    counts[0] = near_count
    counts[1] = far_count

    level_h = lax.broadcasted_iota(jnp.int32, (BLOCKS, BLK), 0)
    level_l = lax.broadcasted_iota(jnp.int32, (BLK, BLK), 0)
    lanes = lax.broadcasted_iota(jnp.int32, (BLOCKS, BLK), 1).astype(F32)
    left = []
    right = []
    for block in range(BLOCKS):
        wanted = order[block : block + 1, :]
        in_high = (level_h == jnp.broadcast_to(wanted >> 7, (BLOCKS, BLK))).astype(F32)
        in_low = (level_l == jnp.broadcast_to(wanted & 127, (BLK, BLK))).astype(F32)
        left.append(jnp.concatenate([in_high * float(block), in_high * lanes], axis=0).astype(BF16))
        right.append(in_low.astype(BF16))
    total = lax.dot_general(
        jnp.concatenate(left, axis=1),
        jnp.concatenate(right, axis=1),
        (((1,), (1,)), ((), ())),
        preferred_element_type=F32,
    )
    inverse[...] = (total[0:BLOCKS] * float(BLK) + total[BLOCKS:]).astype(jnp.int32)


def feature_kernel(type_width, own, after, second, features, vectors):
    level = sublane()
    squares = jnp.zeros((8, BLK), F32)
    for t in range(NTYPES):
        squares = jnp.where(level == t, type_width[t] * type_width[t], squares)
    low3 = level < 3
    low6 = level < 6
    zero = jnp.zeros((8, BLK), F32)
    ones3 = jnp.where(low3, 1.0, 0.0)

    for part, source in enumerate((own, after, second)):

        def one_block(block, part=part, source=source):
            vectors[part * BLOCKS + block] = source[block, 0:VECS, :]
            coded = source[block, VECS:ROWS, :].astype(F32)
            near = coded + pltpu.roll(coded, 5, 0)
            square = near * near
            weight = square[0:1] + square[1:2] + square[2:3] + SOFTENING * SOFTENING
            weight_h, weight_m, weight_l = split3(weight)
            coarse = jnp.where(low3, coded, pltpu.roll(coded, 3, 0)) * -2.0
            fine = jnp.where(low3, pltpu.roll(coded, 5, 0), coded) * -2.0
            own_type = jnp.broadcast_to(coded[6:7], (8, BLK))
            own_square = jnp.zeros((8, BLK), F32)
            for t in range(NTYPES):
                own_square = jnp.where(own_type == float(t), type_width[t] * type_width[t], own_square)
            scale = 1.0 / (own_square + squares)
            scale_h, scale_m, scale_l = split3(jnp.where(low6, scale, 0.0))
            wide = lambda v: jnp.broadcast_to(v, (8, BLK))
            weights = jnp.where(
                level == 0,
                wide(weight_h),
                jnp.where(level == 1, wide(weight_m), jnp.where(level == 2, wide(weight_l), 0.0)),
            )
            stacked = jnp.concatenate(
                [
                    jnp.where(low6, coarse, 0.0),
                    jnp.where(low6, fine, 0.0),
                    jnp.where(low6, coded, 1.0),
                    weights,
                    ones3,
                    zero,
                    scale_h,
                    scale_m,
                    scale_l,
                ]
                + [zero] * 7,
                axis=0,
            )
            features[part * BLOCKS + block] = stacked.astype(BF16).T

        def some_blocks(turn, carry, one_block=one_block):
            for extra in range(16):
                one_block(turn * 16 + extra)
            return carry

        lax.fori_loop(0, BLOCKS // 16, some_blocks, 0)


def row_operands(row_data, operands):
    level = sublane()
    zero = jnp.zeros((8, BLK), F32)

    def some_rows(turn, carry):
        for extra in range(16):
            row = turn * 16 + extra
            coded = row_data[row, VECS:ROWS, :].astype(F32)
            near = coded + pltpu.roll(coded, 5, 0)
            square = near * near
            weight_h, weight_m, weight_l = split3(square[0:1] + square[1:2] + square[2:3])
            wide = lambda v: jnp.broadcast_to(v, (8, BLK))
            weights = jnp.where(
                level == 0,
                wide(weight_h),
                jnp.where(level == 1, wide(weight_m), jnp.where(level == 2, wide(weight_l), 0.0)),
            )
            hot = (level.astype(F32) == wide(coded[6:7])).astype(F32)
            operands[row] = jnp.concatenate(
                [coded, coded, weights, zero, hot, hot, hot, zero], axis=0
            ).astype(BF16)
        return carry

    lax.fori_loop(0, HALF // 16, some_rows, 0)


def pair_products(code, operands, features, step_rows, step_lanes):
    step = (code >> 14) & 255
    right = operands[code & 127]
    empty = jnp.zeros((48, BLK), BF16)
    left = features[(code >> 7) & 127].reshape(8, 16, BLK) + step_lanes[step][None]
    both = jnp.concatenate(
        [
            jnp.concatenate([right[0:16], step_rows[step], right[16:32], empty[0:32]], axis=0),
            jnp.concatenate([empty, right[32:64]], axis=0),
        ],
        axis=1,
    )
    return jnp.dot(left.reshape(BLK, BLK)[:, 0:DEPTH], both, preferred_element_type=F32)


def tile_values(distance2, inverse_spread):
    square = distance2 * inverse_spread
    poly = ERF_COEFFS[-1]
    for coefficient in ERF_COEFFS[-2::-1]:
        poly = poly * square + coefficient
    poly = poly * square
    return (jnp.tanh(poly * lax.rsqrt(poly)) * lax.rsqrt(distance2)).astype(BF16)


def pair_loop(
    phase, counts, codes, row_data, operands, vectors, features, step_rows, step_lanes, row_acc, col_acc, waiting, tiles
):
    base = phase * SLOT_SPAN
    batches = (counts[phase] + UNROLL - 1) // UNROLL

    def one_turn(turn, carry):
        adding = base + jnp.maximum(turn - 2, 0) * UNROLL
        opening = base + jnp.maximum(jnp.minimum(turn, batches - 1), 0) * UNROLL
        sums = []
        for first in range(0, UNROLL, 2):
            done = [codes[0, adding + first + k] for k in range(2)]
            both = [tiles[first + k] for k in range(2)]
            forward = jnp.dot(
                jnp.concatenate([vectors[(code >> 7) & 127] for code in done], axis=0),
                jnp.concatenate(both, axis=1),
                preferred_element_type=F32,
            )
            backward = lax.dot_general(
                jnp.concatenate([row_data[code & 127, 0:VECS, :] for code in done], axis=0),
                jnp.concatenate(both, axis=0),
                (((1,), (1,)), ((), ())),
                preferred_element_type=F32,
            )
            for k, code in enumerate(done):
                to_row = jnp.where(jnp.logical_or(turn < 2, ((code >> 23) & 1) == 1), HALF, code & 127)
                to_col = jnp.where(
                    jnp.logical_or(turn < 2, ((code >> 22) & 1) == 1), COLS, (code >> 7) & 127
                )
                own = (slice(k * VECS, (k + 1) * VECS), slice(k * BLK, (k + 1) * BLK))
                sums.append((to_row, forward[own], to_col, backward[own]))
            for k in range(2):
                slot = first + k
                tiles[slot] = tile_values(waiting[slot, :, 0:BLK], waiting[slot, :, BLK:])
                code = codes[0, opening + slot]
                waiting[slot] = pair_products(code, operands, features, step_rows, step_lanes)
        for to_row, forward, to_col, backward in sums:
            row_acc[to_row] += forward
            col_acc[to_col] += backward
        return carry

    lax.fori_loop(0, batches + 2, one_turn, 0)


def near_far_kernel(phase, *refs):
    counts, codes = refs[0:2]
    pieces = refs[2:6]
    vectors, features, step_rows, step_lanes = refs[6:10]
    col_in = refs[10:11] if phase == 1 else ()
    outs = refs[10 + len(col_in) : -6]
    row_data, operands, row_acc, col_acc, waiting, tiles = refs[-6:]
    position = here()[1] & 3
    for k, piece in enumerate(pieces):
        start = pl.multiple_of(((position - k) & 3) * BLOCKS, BLOCKS)
        row_data[pl.ds(start, BLOCKS)] = piece[...]
    row_operands(row_data, operands)
    row_acc[...] = jnp.zeros_like(row_acc)
    if phase == 0:
        col_acc[...] = jnp.zeros_like(col_acc)
    else:
        col_acc[0:COLS] = col_in[0][...]
    pair_loop(
        phase,
        counts,
        codes,
        row_data,
        operands,
        vectors,
        features,
        step_rows,
        step_lanes,
        row_acc,
        col_acc,
        waiting,
        tiles,
    )
    for k in range(4):
        start = pl.multiple_of(((position + k) & 3) * BLOCKS, BLOCKS)
        outs[k][...] = row_acc[pl.ds(start, BLOCKS)].astype(outs[k].dtype)
    if phase == 0:
        outs[4][...] = col_acc[0:COLS]
    else:
        for step in range(3):
            outs[4 + step][...] = col_acc[step * BLOCKS : (step + 1) * BLOCKS].astype(outs[4 + step].dtype)


def sum_kernel(*refs):
    total = refs[0][...].astype(F32)
    for ref in refs[1:-1]:
        total = total + ref[...].astype(F32)
    refs[-1][...] = total.astype(refs[-1].dtype)


def final_kernel(type_hard, *refs):
    atom_type, krylov, inverse, out_hbm, blocked, out, done = refs[-7:]
    parts = refs[:-7]

    def add_up(turn, carry):
        for extra in range(8):
            block = turn * 8 + extra
            total = parts[0][block]
            for part in parts[1:]:
                total = total + part[block].astype(F32)
            blocked[block] = total
        return carry

    lax.fori_loop(0, BLOCKS // 8, add_up, 0)
    saves = []
    for chunk in range(BLOCKS):
        wanted = jnp.broadcast_to(inverse[chunk : chunk + 1, :], (8, BLK))
        source = wanted >> 7
        lane = wanted & 127
        span = slice(chunk * BLK, (chunk + 1) * BLK)
        kind = jnp.broadcast_to(atom_type[:, span], (8, BLK))
        hard = jnp.zeros((8, BLK), F32)
        for t in range(NTYPES):
            hard = jnp.where(kind == t, type_hard[t], hard)
        top = jnp.zeros((8, BLK), F32)
        low = jnp.zeros((8, BLK), F32)
        for block in range(BLOCKS):
            top = jnp.where(source == block, lane_gather(blocked[block, 0:8, :], lane), top)
            low = jnp.where(source == block, lane_gather(blocked[block, 8:16, :], lane), low)
        out[0:8, span] = top + hard * krylov[0:8, span]
        out[8:16, span] = low + hard * krylov[8:16, span]
        if chunk % 8 == 7:
            group = slice((chunk - 7) * BLK, (chunk + 1) * BLK)
            save = pltpu.make_async_copy(out.at[:, group], out_hbm.at[:, group], done.at[chunk // 8])
            save.start()
            saves.append(save)
    for save in saves:
        save.wait()


def shape(dims, dtype):
    return jax.ShapeDtypeStruct(dims, dtype)


def call(kernel, out_shape, in_specs, out_specs, name, scratch=(), vmem=20, cost=None):
    return pl.pallas_call(
        kernel,
        out_shape=out_shape,
        in_specs=in_specs,
        out_specs=out_specs,
        scratch_shapes=list(scratch),
        compiler_params=pltpu.CompilerParams(vmem_limit_bytes=vmem << 20),
        cost_estimate=cost,
        name=name,
    )


def step_tables():
    x, y, z = np.meshgrid(np.arange(3), np.arange(-4, 5), np.arange(-2, 3), indexing="ij")
    steps = np.stack([x, y, z], axis=-1).reshape(-1, 3) * np.array(CELL)
    squared = np.sum(steps * steps, axis=1).astype(np.float32)
    coarse = squared.astype(ml_dtypes.bfloat16).astype(np.float32)
    rows = np.zeros((len(steps), 16, BLK), np.float32)
    rows[:, 0:3] = rows[:, 3:6] = 2.0 * steps[:, :, None]
    rows[:, 6] = coarse[:, None]
    rows[:, 7] = (squared - coarse)[:, None]
    rows[:, 8:11] = 1.0
    lanes = np.zeros((len(steps), 16, BLK), np.float32)
    lanes[:, :, 0:3] = lanes[:, :, 3:6] = -2.0 * steps[:, None, :]
    return rows.astype(ml_dtypes.bfloat16), lanes.astype(ml_dtypes.bfloat16)


def passed_down(value, steps):
    count = lax.axis_size("row")
    return lax.ppermute(value, "row", [(s, s - steps) for s in range(steps, count)])


def passed_up(value, steps):
    count = lax.axis_size("row")
    return lax.ppermute(value, "row", [(s, s + steps) for s in range(count - steps)])


def across(value):
    return lax.ppermute(value, "col", [(c, c ^ 4) for c in range(8)])


def around(value, steps):
    return lax.ppermute(value, "col", [(c, (c & 4) + (c + steps) % 4) for c in range(8)])


def on_device(
    positions, atom_type, krylov, block_order, type_width, type_hard, pair_rows, pair_cols, pair_count
):
    order = block_order.reshape(BLOCKS, BLK)
    kinds = atom_type.reshape(1, -1)

    packed = call(
        prep_kernel,
        shape((BLOCKS, ROWS, BLK), BF16),
        [ANY, ANY, ANY, ANY],
        VMEM,
        "prep",
        scratch=[
            pltpu.VMEM((8, BLOCKS // 2 * BLK), F32),
            pltpu.VMEM((3, BLOCKS * BLK), F32),
            pltpu.VMEM((1, BLOCKS * BLK), jnp.int32),
            pltpu.VMEM((VECS, BLOCKS * BLK), F32),
            pltpu.VMEM((BLOCKS, BLK), jnp.int32),
            pltpu.SemaphoreType.DMA((4,)),
        ],
        vmem=62,
    )(positions, kinds, krylov, order)

    other = across(packed)
    after = passed_down(packed, 1)
    second = passed_down(packed, 2)
    rows_list, _ = lax.optimization_barrier((pair_rows.reshape(1, SLOTS), packed))

    inverse, codes, counts = call(
        side_kernel,
        (
            shape((BLOCKS, BLK), jnp.int32),
            shape((1, 2 * SLOT_SPAN), jnp.int32),
            shape((2,), jnp.int32),
        ),
        [ANY, ANY, ANY, ANY],
        (VMEM, VMEM, SMEM),
        "side",
        scratch=[
            pltpu.SMEM((1, 1), jnp.int32),
            pltpu.VMEM((1, SLOTS), jnp.int32),
            pltpu.VMEM((1, SLOTS), jnp.int32),
            pltpu.VMEM((BLOCKS, BLK), jnp.int32),
            pltpu.SemaphoreType.DMA((4,)),
        ],
        vmem=62,
        cost=time_cost(2),
    )(pair_count, rows_list, pair_cols.reshape(1, SLOTS), order)

    near_rows = [packed] + [around(packed, k) for k in (1, 2, 3)]

    features, vectors = call(
        feature_kernel,
        (shape((COLS, BLK, BLK), BF16), shape((COLS, VECS, BLK), BF16)),
        [SMEM, VMEM, VMEM, VMEM],
        (VMEM, VMEM),
        "features",
        cost=time_cost(12),
    )(type_width, packed, after, second)

    far_rows = [other] + [around(other, k) for k in (1, 2, 3)]
    step_rows, step_lanes = step_tables()
    codes, _ = lax.optimization_barrier((codes, other))
    scratch = [
        pltpu.VMEM((HALF, ROWS, BLK), BF16),
        pltpu.VMEM((HALF, 64, BLK), BF16),
        pltpu.VMEM((HALF + 1, VECS, BLK), F32),
        pltpu.VMEM((COLS + 1, VECS, BLK), F32),
        pltpu.VMEM((UNROLL, BLK, 2 * BLK), F32),
        pltpu.VMEM((UNROLL, BLK, BLK), BF16),
    ]
    block_set = (BLOCKS, VECS, BLK)
    *near_sums, col_sums = call(
        functools.partial(near_far_kernel, 0),
        [shape(block_set, F32)] + [shape(block_set, BF16)] * 3 + [shape((COLS, VECS, BLK), F32)],
        [SMEM] * 2 + [VMEM] * 8,
        [VMEM] * 5,
        "pairs_near",
        scratch=scratch,
        cost=PAIR_COST,
    )(counts, codes, *near_rows, vectors, features, step_rows, step_lanes)

    *far_sums, own_sum, after_sum, last_sum = call(
        functools.partial(near_far_kernel, 1),
        [shape(block_set, BF16)] * 4 + [shape(block_set, F32)] + [shape(block_set, BF16)] * 2,
        [SMEM] * 2 + [VMEM] * 9,
        [VMEM] * 7,
        "pairs_far",
        scratch=scratch,
        cost=PAIR_COST,
    )(counts, codes, *far_rows, vectors, features, step_rows, step_lanes, col_sums)

    far_parts = [far_sums[0]] + [around(far_sums[k], k) for k in (1, 2, 3)]
    from_prior = passed_up(after_sum, 1)
    from_second = passed_up(last_sum, 2)
    far_sum = call(
        sum_kernel, shape((BLOCKS, VECS, BLK), BF16), [VMEM] * 4, VMEM, "far_sum"
    )(*far_parts)
    from_far = across(far_sum)
    near_sums, _ = lax.optimization_barrier((near_sums, (far_sum, from_prior, from_second)))
    near_parts = [near_sums[0]] + [around(near_sums[k], k) for k in (1, 2, 3)]

    parts = [own_sum, from_far, from_prior, from_second, *near_parts]
    return call(
        final_kernel,
        shape(krylov.shape, F32),
        [SMEM] + [VMEM] * (len(parts) + 3),
        ANY,
        "final",
        scratch=[
            pltpu.VMEM((BLOCKS, VECS, BLK), F32),
            pltpu.VMEM((VECS, BLOCKS * BLK), F32),
            pltpu.SemaphoreType.DMA((4,)),
        ],
    )(type_hard, *parts, kinds, krylov, inverse)


def solution(mesh):
    placed = (
        P(None, ("row", "col")),
        P(("row", "col")),
        P(None, ("row", "col")),
        P(("row", "col")),
        P(),
        P(),
        P("row", "col", None),
        P("row", "col", None),
        P("row", "col"),
    )
    return jax.shard_map(
        on_device, mesh=mesh, in_specs=placed, out_specs=P(None, ("row", "col")), check_vma=False
    )
```

profile of v0, /device:TPU:49, one launch (start us, length us, event | category | flops | bytes accessed | tf_op | source)
XLA Modules:
  0.0 95.7 jit_solution(7701937971973403317)
XLA Ops:
  0.0 3.7 %prep.1.own.refs_2_ = bf16[32,24,128]{2,1,0:T(8,128)(2,1)} custom-call(f32[3,4096]{1,0:T(4,128)} %positions_hbm.1, s32[1,4096]{1,0:T(1,128)} %bitcast.4, f32[16,4096]{1,0:T(8,128)} %refs_9_.3, s32[32,128]{1,0:T(8,128)} %bitcast.6), custom_call_target="tpu_custom_call" | custom-call | tf_op jit(solution)/shard_map/prep/pallas_call | solution.py:515
  3.7 3.9 %collective-permute-start.5 = (bf16[32,24,128]{2,1,0:T(8,128)(2,1)}, bf16[32,24,128]{2,1,0:T(8,128)(2,1)S(1)}, u32[]{:S(2)}, u32[]{:S(2)}) collective-permute-start(bf16[32,24,128]{2,1,0:T(8,128)(2,1)} %prep.1.own.refs_2_), channel_id=1, source_target_pairs={{16,0},{24,8},{32,16},{40,24},{48,32},{56,40},{64,48},{72,56},{80,... | collective-permute-start | bytes 589832 | tf_op jit(solution)/shard_map/ppermute | solution.py:493
  7.6 7.0 %collective-permute-start = (bf16[32,24,128]{2,1,0:T(8,128)(2,1)}, bf16[32,24,128]{2,1,0:T(8,128)(2,1)S(1)}, u32[]{:S(2)}, u32[]{:S(2)}) collective-permute-start(bf16[32,24,128]{2,1,0:T(8,128)(2,1)} %prep.1.own.refs_2_), channel_id=1, source_target_pairs={{0,4},{1,5},{2,6},{3,7},{4,0},{5,1},{6,2},{7,3},{8,12},{9,13},{10,... | collective-permute-start | bytes 589832 | tf_op jit(solution)/shard_map/ppermute | solution.py:502
  14.6 3.1 %collective-permute-start.4 = (bf16[32,24,128]{2,1,0:T(8,128)(2,1)}, bf16[32,24,128]{2,1,0:T(8,128)(2,1)S(1)}, u32[]{:S(2)}, u32[]{:S(2)}) collective-permute-start(bf16[32,24,128]{2,1,0:T(8,128)(2,1)} %prep.1.own.refs_2_), channel_id=1, source_target_pairs={{8,0},{16,8},{24,16},{32,24},{40,32},{48,40},{56,48},{64,56},{72,6... | collective-permute-start | bytes 589832 | tf_op jit(solution)/shard_map/ppermute | solution.py:493
  17.8 0.2 collective-permute-start.8
  18.0 2.6 %collective-permute-start.7 = (bf16[32,24,128]{2,1,0:T(8,128)(2,1)}, bf16[32,24,128]{2,1,0:T(8,128)(2,1)S(1)}, u32[]{:S(2)}, u32[]{:S(2)}) collective-permute-start(bf16[32,24,128]{2,1,0:T(8,128)(2,1)} %prep.1.own.refs_2_), channel_id=1, source_target_pairs={{0,2},{1,3},{2,0},{3,1},{4,6},{5,7},{6,4},{7,5},{8,10},{9,11},{10,... | collective-permute-start | bytes 589832 | tf_op jit(solution)/shard_map/ppermute | solution.py:506
  21.3 0.0 copy-start.5
  21.3 2.5 %side.1 = (s32[32,128]{1,0:T(8,128)}, s32[1,1280]{1,0:T(1,128)}, s32[2]{0:T(128)}) custom-call(s32[1,1]{1,0:T(1,128)S(6)} %copy.12.count_hbm, s32[1,512]{1,0:T(1,128)} %bitcast.8, s32[1,512]{1,0:T(1,128)} %bitcast.9, s32[32,128]{1,0:T(8,128)} %bitcast.7), custom_call_target="tpu_custom_call" | custom-call | flops 2000000000 | bytes 1000000 | tf_op jit(solution)/shard_map/side/pallas_call | solution.py:537
  23.8 0.0 copy-start.6
  23.8 0.0 copy-start.7
  23.8 0.1 collective-permute-start.6
  23.9 2.9 %collective-permute-done.refs_2_ = bf16[32,24,128]{2,1,0:T(8,128)(2,1)S(1)} collective-permute-done((bf16[32,24,128]{2,1,0:T(8,128)(2,1)}, bf16[32,24,128]{2,1,0:T(8,128)(2,1)S(1)}, u32[]{:S(2)}, u32[]{:S(2)}) %collective-permute-start) | collective-permute-done | bytes 196640 | tf_op jit(solution)/shard_map/ppermute | solution.py:502
  26.8 0.2 collective-permute-start.3
  27.0 2.6 %collective-permute-start.2 = (bf16[32,24,128]{2,1,0:T(8,128)(2,1)S(1)}, bf16[32,24,128]{2,1,0:T(8,128)(2,1)S(1)}, u32[]{:S(2)}, u32[]{:S(2)}) collective-permute-start(bf16[32,24,128]{2,1,0:T(8,128)(2,1)S(1)} %collective-permute-done.refs_2_), channel_id=1, source_target_pairs={{0,2},{1,3},{2,0},{3,1},{4,6},{5,7},{6,4},{7,5},{8,10},{9,11},{10,... | collective-permute-start | bytes 589832 | tf_op jit(solution)/shard_map/ppermute | solution.py:506
  29.6 1.9 %features.1 = (bf16[96,128,128]{2,1,0:T(8,128)(2,1)S(1)}, bf16[96,16,128]{2,1,0:T(8,128)(2,1)S(1)}) custom-call(f32[6]{0:T(128)S(1)} %copy-done.5, bf16[32,24,128]{2,1,0:T(8,128)(2,1)S(1)} %copy-done.1, bf16[32,24,128]{2,1,0:T(8,128)(2,1)S(1)} %collective-permute-done.4.after, bf16[32,24,128]{2,1,0:T(8,128)(2,1)S(1)} %collective-permute-done.5.second), custom_call_target="tpu_custom_call" | custom-call | flops 12000000000 | bytes 1000000 | tf_op jit(solution)/shard_map/features/pallas_call | solution.py:560
  31.5 0.1 collective-permute-start.1
  31.7 12.7 %pairs_near.1 = (f32[32,16,128]{2,1,0:T(8,128)S(1)}, bf16[32,16,128]{2,1,0:T(8,128)(2,1)S(1)}, bf16[32,16,128]{2,1,0:T(8,128)(2,1)S(1)}, bf16[32,16,128]{2,1,0:T(8,128)(2,1)S(1)}, f32[96,16,128]{2,1,0:T(8,128)S(1)}) custom-call(s32[2]{0:T(128)S(1)} %copy-done.9, s32[1,1280]{1,0:T(1,128)S(1)} %copy-done.8, bf16[32,24,128]{2,1,0:T(8,128)(2,1)S(1)} %copy-done.1, ...), custom_call_target="tpu_custom_call" | custom-call | flops 16000000000 | bytes 1000000 | tf_op jit(solution)/shard_map/pairs_near/pallas_call | solution.py:581
  44.4 0.0 copy-start
  44.4 0.0 copy-start.2
  44.5 0.0 copy-start.4
  44.5 8.1 %pairs_far.1 = (bf16[32,16,128]{2,1,0:T(8,128)(2,1)S(1)}, bf16[32,16,128]{2,1,0:T(8,128)(2,1)S(1)}, bf16[32,16,128]{2,1,0:T(8,128)(2,1)S(1)}, bf16[32,16,128]{2,...) custom-call(s32[2]{0:T(128)S(1)} %copy-done.9, ...), custom_call_target="tpu_custom_call" | custom-call | flops 16000000000 | bytes 1000000 | tf_op jit(solution)/shard_map/pairs_far/pallas_call | solution.py:591
  52.6 4.4 %collective-permute-start.9 = (bf16[32,16,128]{2,1,0:T(8,128)(2,1)S(1)}, bf16[32,16,128]{2,1,0:T(8,128)(2,1)S(1)}, u32[]{:S(2)}, u32[]{:S(2)}) collective-permute-start(bf16[32,16,128]{2,1,0:T(8,128)(2,1)S(1)} %get-tuple-element.37), channel_id=1, source_target_pairs={{0,1},{1,2},{2,3},{3,0},{4,5},{5,6},{6,7},{7,4},{8,9},{9,10},{10,1... | collective-permute-start | bytes 393224 | tf_op jit(solution)/shard_map/ppermute | solution.py:506
  57.0 6.9 %collective-permute-start.10 = (bf16[32,16,128]{2,1,0:T(8,128)(2,1)S(1)}, bf16[32,16,128]{2,1,0:T(8,128)(2,1)S(1)}, u32[]{:S(2)}, u32[]{:S(2)}) collective-permute-start(bf16[32,16,128]{2,1,0:T(8,128)(2,1)S(1)} %get-tuple-element.38), channel_id=1, source_target_pairs={{0,2},{1,3},{2,0},{3,1},{4,6},{5,7},{6,4},{7,5},{8,10},{9,11},{10,... | collective-permute-start | bytes 393224 | tf_op jit(solution)/shard_map/ppermute | solution.py:506
  63.8 5.7 %collective-permute-start.13 = (bf16[32,16,128]{2,1,0:T(8,128)(2,1)S(1)}, bf16[32,16,128]{2,1,0:T(8,128)(2,1)S(1)}, u32[]{:S(2)}, u32[]{:S(2)}) collective-permute-start(bf16[32,16,128]{2,1,0:T(8,128)(2,1)S(1)} %get-tuple-element.40), channel_id=1, source_target_pairs={{0,8},{8,16},{16,24},{24,32},{32,40},{40,48},{48,56},{56,64},{64,7... | collective-permute-start | bytes 393224 | tf_op jit(solution)/shard_map/ppermute | solution.py:498
  69.5 1.9 %collective-permute-start.14 = (bf16[32,16,128]{2,1,0:T(8,128)(2,1)S(1)}, bf16[32,16,128]{2,1,0:T(8,128)(2,1)S(1)}, u32[]{:S(2)}, u32[]{:S(2)}) collective-permute-start(bf16[32,16,128]{2,1,0:T(8,128)(2,1)S(1)} %get-tuple-element.41), channel_id=1, source_target_pairs={{0,16},{8,24},{16,32},{24,40},{32,48},{40,56},{48,64},{56,72},{64,... | collective-permute-start | bytes 393224 | tf_op jit(solution)/shard_map/ppermute | solution.py:498
  71.5 0.1 far_sum.1
  71.6 0.1 collective-permute-start.12
  71.7 10.1 %collective-permute-done.14.refs_3_ = bf16[32,16,128]{2,1,0:T(8,128)(2,1)S(1)} collective-permute-done((bf16[32,16,128]{2,1,0:T(8,128)(2,1)S(1)}, bf16[32,16,128]{2,1,0:T(8,128)(2,1)S(1)}, u32[]{:S(2)}, u32[]{:S(2)}) %collective-permute-start.14) | collective-permute-done | bytes 131104 | tf_op jit(solution)/shard_map/ppermute | solution.py:498
  81.8 1.5 %collective-permute-start.17 = (bf16[32,16,128]{2,1,0:T(8,128)(2,1)S(1)}, bf16[32,16,128]{2,1,0:T(8,128)(2,1)S(1)}, u32[]{:S(2)}, u32[]{:S(2)}) collective-permute-start(bf16[32,16,128]{2,1,0:T(8,128)(2,1)S(1)} %get-tuple-element.49), channel_id=1, source_target_pairs={{0,3},{1,0},{2,1},{3,2},{4,7},{5,4},{6,5},{7,6},{8,11},{9,8},{10,9... | collective-permute-start | bytes 393224 | tf_op jit(solution)/shard_map/ppermute | solution.py:506
  83.3 6.6 %collective-permute-done.15.refs_5_ = bf16[32,16,128]{2,1,0:T(8,128)(2,1)S(1)} collective-permute-done((bf16[32,16,128]{2,1,0:T(8,128)(2,1)S(1)}, bf16[32,16,128]{2,1,0:T(8,128)(2,1)S(1)}, u32[]{:S(2)}, u32[]{:S(2)}) %collective-permute-start.15) | collective-permute-done | bytes 131104 | tf_op jit(solution)/shard_map/ppermute | solution.py:506
  89.9 2.0 %collective-permute-done.17.refs_7_ = bf16[32,16,128]{2,1,0:T(8,128)(2,1)S(1)} collective-permute-done((bf16[32,16,128]{2,1,0:T(8,128)(2,1)S(1)}, bf16[32,16,128]{2,1,0:T(8,128)(2,1)S(1)}, u32[]{:S(2)}, u32[]{:S(2)}) %collective-permute-start.17) | collective-permute-done | bytes 131104 | tf_op jit(solution)/shard_map/ppermute | solution.py:506
  91.9 3.7 %final.1 = f32[16,4096]{1,0:T(8,128)} custom-call(f32[6]{0:T(128)S(1)} %copy-done.4, f32[32,16,128]{2,1,0:T(8,128)S(1)} %get-tuple-element.35.refs_0_, bf16[32,16,128]{2,1,0:T(8,128)(2,1)S(1)} %collective-permute-done.12.refs_1_, bf16[32,16,128]{2,1,0:T(8,128)(2,1)S(1)} %collective-permute-done.13.refs_2_, ...), custom_call_target="tpu_custom_call" | custom-call | tf_op jit(solution)/shard_map/final/pallas_call | solution.py:612
  (31 shorter events, 0.1 us)
Async XLA Ops:
  3.7 20.1 %collective-permute-start.5 = (bf16[32,24,128]{2,1,0:T(8,128)(2,1)}, bf16[32,24,128]{2,1,0:T(8,128)(2,1)S(1)}, u32[]{:S(2)}, u32[]{:S(2)}) collective-permute-start(bf16[32,24,128]{2,1,0:T(8,128)(2,1)} %prep.1.own.refs_2_), channel_id=1, source_target_pairs={{16,0},{24,8},{32,16},{40,24},{48,32},{56,40},{64,48},{72,56},{80,... | collective-permute-start | bytes 589832 | tf_op jit(solution)/shard_map/ppermute | solution.py:493
  7.6 19.2 %collective-permute-start = (bf16[32,24,128]{2,1,0:T(8,128)(2,1)}, bf16[32,24,128]{2,1,0:T(8,128)(2,1)S(1)}, u32[]{:S(2)}, u32[]{:S(2)}) collective-permute-start(bf16[32,24,128]{2,1,0:T(8,128)(2,1)} %prep.1.own.refs_2_), channel_id=1, source_target_pairs={{0,4},{1,5},{2,6},{3,7},{4,0},{5,1},{6,2},{7,3},{8,12},{9,13},{10,... | collective-permute-start | bytes 589832 | tf_op jit(solution)/shard_map/ppermute | solution.py:502
  14.6 12.4 %collective-permute-start.4 = (bf16[32,24,128]{2,1,0:T(8,128)(2,1)}, bf16[32,24,128]{2,1,0:T(8,128)(2,1)S(1)}, u32[]{:S(2)}, u32[]{:S(2)}) collective-permute-start(bf16[32,24,128]{2,1,0:T(8,128)(2,1)} %prep.1.own.refs_2_), channel_id=1, source_target_pairs={{8,0},{16,8},{24,16},{32,24},{40,32},{48,40},{56,48},{64,56},{72,6... | collective-permute-start | bytes 589832 | tf_op jit(solution)/shard_map/ppermute | solution.py:493
  17.8 13.8 %collective-permute-start.8 = (bf16[32,24,128]{2,1,0:T(8,128)(2,1)}, bf16[32,24,128]{2,1,0:T(8,128)(2,1)S(1)}, u32[]{:S(2)}, u32[]{:S(2)}) collective-permute-start(bf16[32,24,128]{2,1,0:T(8,128)(2,1)} %prep.1.own.refs_2_), channel_id=1, source_target_pairs={{0,3},{1,0},{2,1},{3,2},{4,7},{5,4},{6,5},{7,6},{8,11},{9,8},{10,9... | collective-permute-start | bytes 589832 | tf_op jit(solution)/shard_map/ppermute | solution.py:506
  18.0 13.6 %collective-permute-start.7 = (bf16[32,24,128]{2,1,0:T(8,128)(2,1)}, bf16[32,24,128]{2,1,0:T(8,128)(2,1)S(1)}, u32[]{:S(2)}, u32[]{:S(2)}) collective-permute-start(bf16[32,24,128]{2,1,0:T(8,128)(2,1)} %prep.1.own.refs_2_), channel_id=1, source_target_pairs={{0,2},{1,3},{2,0},{3,1},{4,6},{5,7},{6,4},{7,5},{8,10},{9,11},{10,... | collective-permute-start | bytes 589832 | tf_op jit(solution)/shard_map/ppermute | solution.py:506
  21.3 2.6 %copy-start.1 = (bf16[32,24,128]{2,1,0:T(8,128)(2,1)S(1)}, bf16[32,24,128]{2,1,0:T(8,128)(2,1)}, u32[]{:S(2)}) copy-start(bf16[32,24,128]{2,1,0:T(8,128)(2,1)} %prep.1.own.refs_2_) | copy-start | bytes 589828
  21.3 8.3 %copy-start.5 = (f32[6]{0:T(128)S(1)}, f32[6]{0:T(128)}, u32[]{:S(2)}) copy-start(f32[6]{0:T(128)} %type_width.1) | copy-start | bytes 76
  23.8 7.9 %copy-start.6 = (bf16[135,16,128]{2,1,0:T(8,128)(2,1)S(1)}, bf16[135,16,128]{2,1,0:T(8,128)(2,1)}, u32[]{:S(2)}) copy-start(bf16[135,16,128]{2,1,0:T(8,128)(2,1)} %constant.5.clone.refs_9_) | copy-start | bytes 1658884
  23.8 7.9 %copy-start.7 = (bf16[135,16,128]{2,1,0:T(8,128)(2,1)S(1)}, bf16[135,16,128]{2,1,0:T(8,128)(2,1)}, u32[]{:S(2)}) copy-start(bf16[135,16,128]{2,1,0:T(8,128)(2,1)} %constant.4.clone.refs_8_) | copy-start | bytes 1658884
  23.8 7.9 %copy-start.8 = (s32[1,1280]{1,0:T(1,128)S(1)}, s32[1,1280]{1,0:T(1,128)}, u32[]{:S(2)}) copy-start(s32[1,1280]{1,0:T(1,128)} %get-tuple-element.31.refs_1_) | copy-start | bytes 15364
  23.8 7.9 %copy-start.9 = (s32[2]{0:T(128)S(1)}, s32[2]{0:T(128)}, u32[]{:S(2)}) copy-start(s32[2]{0:T(128)} %get-tuple-element.29.refs_0_) | copy-start | bytes 28
  23.8 7.8 %collective-permute-start.6 = (bf16[32,24,128]{2,1,0:T(8,128)(2,1)S(1)}, bf16[32,24,128]{2,1,0:T(8,128)(2,1)S(1)}, u32[]{:S(2)}, u32[]{:S(2)}) collective-permute-start(bf16[32,24,128]{2,1,0:T(8,128)(2,1)S(1)} %copy-done.1), channel_id=1, source_target_pairs={{0,1},{1,2},{2,3},{3,0},{4,5},{5,6},{6,7},{7,4},{8,9},{9,10},{10,1... | collective-permute-start | bytes 589832 | tf_op jit(solution)/shard_map/ppermute | solution.py:506
  26.8 17.6 %collective-permute-start.3 = (bf16[32,24,128]{2,1,0:T(8,128)(2,1)S(1)}, bf16[32,24,128]{2,1,0:T(8,128)(2,1)S(1)}, u32[]{:S(2)}, u32[]{:S(2)}) collective-permute-start(bf16[32,24,128]{2,1,0:T(8,128)(2,1)S(1)} %collective-permute-done.refs_2_), channel_id=1, source_target_pairs={{0,3},{1,0},{2,1},{3,2},{4,7},{5,4},{6,5},{7,6},{8,11},{9,8},{10,9... | collective-permute-start | bytes 589832 | tf_op jit(solution)/shard_map/ppermute | solution.py:506
  27.0 17.4 %collective-permute-start.2 = (bf16[32,24,128]{2,1,0:T(8,128)(2,1)S(1)}, bf16[32,24,128]{2,1,0:T(8,128)(2,1)S(1)}, u32[]{:S(2)}, u32[]{:S(2)}) collective-permute-start(bf16[32,24,128]{2,1,0:T(8,128)(2,1)S(1)} %collective-permute-done.refs_2_), channel_id=1, source_target_pairs={{0,2},{1,3},{2,0},{3,1},{4,6},{5,7},{6,4},{7,5},{8,10},{9,11},{10,... | collective-permute-start | bytes 589832 | tf_op jit(solution)/shard_map/ppermute | solution.py:506
  31.5 12.9 %collective-permute-start.1 = (bf16[32,24,128]{2,1,0:T(8,128)(2,1)S(1)}, bf16[32,24,128]{2,1,0:T(8,128)(2,1)S(1)}, u32[]{:S(2)}, u32[]{:S(2)}) collective-permute-start(bf16[32,24,128]{2,1,0:T(8,128)(2,1)S(1)} %collective-permute-done.refs_2_), channel_id=1, source_target_pairs={{0,1},{1,2},{2,3},{3,0},{4,5},{5,6},{6,7},{7,4},{8,9},{9,10},{10,1... | collective-permute-start | bytes 589832 | tf_op jit(solution)/shard_map/ppermute | solution.py:506
  44.4 47.4 %copy-start = (f32[16,4096]{1,0:T(8,128)S(1)}, f32[16,4096]{1,0:T(8,128)}, u32[]{:S(2)}) copy-start(f32[16,4096]{1,0:T(8,128)} %refs_9_.3) | copy-start | bytes 786436
  44.4 47.4 %copy-start.2 = (s32[4096]{0:T(1024)S(1)}, s32[4096]{0:T(1024)}, u32[]{:S(2)}) copy-start(s32[4096]{0:T(1024)} %param.12) | copy-start | bytes 49156
  44.5 47.4 %copy-start.3 = (s32[32,128]{1,0:T(8,128)S(1)}, s32[32,128]{1,0:T(8,128)}, u32[]{:S(2)}) copy-start(s32[32,128]{1,0:T(8,128)} %get-tuple-element.50.refs_10_) | copy-start | bytes 49156
  44.5 47.4 %copy-start.4 = (f32[6]{0:T(128)S(1)}, f32[6]{0:T(128)}, u32[]{:S(2)}) copy-start(f32[6]{0:T(128)} %type_hard.1) | copy-start | bytes 76
  52.6 18.9 %collective-permute-start.9 = (bf16[32,16,128]{2,1,0:T(8,128)(2,1)S(1)}, bf16[32,16,128]{2,1,0:T(8,128)(2,1)S(1)}, u32[]{:S(2)}, u32[]{:S(2)}) collective-permute-start(bf16[32,16,128]{2,1,0:T(8,128)(2,1)S(1)} %get-tuple-element.37), channel_id=1, source_target_pairs={{0,1},{1,2},{2,3},{3,0},{4,5},{5,6},{6,7},{7,4},{8,9},{9,10},{10,1... | collective-permute-start | bytes 393224 | tf_op jit(solution)/shard_map/ppermute | solution.py:506
  57.0 14.5 %collective-permute-start.10 = (bf16[32,16,128]{2,1,0:T(8,128)(2,1)S(1)}, bf16[32,16,128]{2,1,0:T(8,128)(2,1)S(1)}, u32[]{:S(2)}, u32[]{:S(2)}) collective-permute-start(bf16[32,16,128]{2,1,0:T(8,128)(2,1)S(1)} %get-tuple-element.38), channel_id=1, source_target_pairs={{0,2},{1,3},{2,0},{3,1},{4,6},{5,7},{6,4},{7,5},{8,10},{9,11},{10,... | collective-permute-start | bytes 393224 | tf_op jit(solution)/shard_map/ppermute | solution.py:506
  63.8 7.6 %collective-permute-start.11 = (bf16[32,16,128]{2,1,0:T(8,128)(2,1)S(1)}, bf16[32,16,128]{2,1,0:T(8,128)(2,1)S(1)}, u32[]{:S(2)}, u32[]{:S(2)}) collective-permute-start(bf16[32,16,128]{2,1,0:T(8,128)(2,1)S(1)} %get-tuple-element.39), channel_id=1, source_target_pairs={{0,3},{1,0},{2,1},{3,2},{4,7},{5,4},{6,5},{7,6},{8,11},{9,8},{10,9... | collective-permute-start | bytes 393224 | tf_op jit(solution)/shard_map/ppermute | solution.py:506
  63.8 7.8 %collective-permute-start.13 = (bf16[32,16,128]{2,1,0:T(8,128)(2,1)S(1)}, bf16[32,16,128]{2,1,0:T(8,128)(2,1)S(1)}, u32[]{:S(2)}, u32[]{:S(2)}) collective-permute-start(bf16[32,16,128]{2,1,0:T(8,128)(2,1)S(1)} %get-tuple-element.40), channel_id=1, source_target_pairs={{0,8},{8,16},{16,24},{24,32},{32,40},{40,48},{48,56},{56,64},{64,7... | collective-permute-start | bytes 393224 | tf_op jit(solution)/shard_map/ppermute | solution.py:498
  69.5 12.3 %collective-permute-start.14 = (bf16[32,16,128]{2,1,0:T(8,128)(2,1)S(1)}, bf16[32,16,128]{2,1,0:T(8,128)(2,1)S(1)}, u32[]{:S(2)}, u32[]{:S(2)}) collective-permute-start(bf16[32,16,128]{2,1,0:T(8,128)(2,1)S(1)} %get-tuple-element.41), channel_id=1, source_target_pairs={{0,16},{8,24},{16,32},{24,40},{32,48},{40,56},{48,64},{56,72},{64,... | collective-permute-start | bytes 393224 | tf_op jit(solution)/shard_map/ppermute | solution.py:498
  71.6 11.7 %collective-permute-start.12 = (bf16[32,16,128]{2,1,0:T(8,128)(2,1)S(1)}, bf16[32,16,128]{2,1,0:T(8,128)(2,1)S(1)}, u32[]{:S(2)}, u32[]{:S(2)}) collective-permute-start(bf16[32,16,128]{2,1,0:T(8,128)(2,1)S(1)} %far_sum.1), channel_id=1, source_target_pairs={{0,4},{1,5},{2,6},{3,7},{4,0},{5,1},{6,2},{7,3},{8,12},{9,13},{10,... | collective-permute-start | bytes 393224 | tf_op jit(solution)/shard_map/ppermute | solution.py:502
  81.8 8.1 %collective-permute-start.15 = (bf16[32,16,128]{2,1,0:T(8,128)(2,1)S(1)}, bf16[32,16,128]{2,1,0:T(8,128)(2,1)S(1)}, u32[]{:S(2)}, u32[]{:S(2)}) collective-permute-start(bf16[32,16,128]{2,1,0:T(8,128)(2,1)S(1)} %get-tuple-element.47), channel_id=1, source_target_pairs={{0,1},{1,2},{2,3},{3,0},{4,5},{5,6},{6,7},{7,4},{8,9},{9,10},{10,1... | collective-permute-start | bytes 393224 | tf_op jit(solution)/shard_map/ppermute | solution.py:506
  81.8 8.1 %collective-permute-start.16 = (bf16[32,16,128]{2,1,0:T(8,128)(2,1)S(1)}, bf16[32,16,128]{2,1,0:T(8,128)(2,1)S(1)}, u32[]{:S(2)}, u32[]{:S(2)}) collective-permute-start(bf16[32,16,128]{2,1,0:T(8,128)(2,1)S(1)} %get-tuple-element.48), channel_id=1, source_target_pairs={{0,2},{1,3},{2,0},{3,1},{4,6},{5,7},{6,4},{7,5},{8,10},{9,11},{10,... | collective-permute-start | bytes 393224 | tf_op jit(solution)/shard_map/ppermute | solution.py:506
  81.8 10.1 %collective-permute-start.17 = (bf16[32,16,128]{2,1,0:T(8,128)(2,1)S(1)}, bf16[32,16,128]{2,1,0:T(8,128)(2,1)S(1)}, u32[]{:S(2)}, u32[]{:S(2)}) collective-permute-start(bf16[32,16,128]{2,1,0:T(8,128)(2,1)S(1)} %get-tuple-element.49), channel_id=1, source_target_pairs={{0,3},{1,0},{2,1},{3,2},{4,7},{5,4},{6,5},{7,6},{8,11},{9,8},{10,9... | collective-permute-start | bytes 393224 | tf_op jit(solution)/shard_map/ppermute | solution.py:506
where the time goes:
time: 95 us; the launch traced here: 95.7 us
  starting transfers between devices  40.3 us (42%)
  Pallas kernels  32.6 us (34%)
  waiting for transfers between devices  21.7 us (23%)
  between operations  1.14 us (1%)
    ppermute x12, starting transfers between devices, around(): lax.ppermute(value, 'col', [(c, (c & 4) + (c + steps) % 4) for c in range...  18.5 us
    pallas_call x1, Pallas kernels, on_device(): call(functools.partial(near_far_kernel, 0), [shape(block_set, F32)] + [sh...  12.7 us
    ppermute x2, waiting for transfers between devices, passed_up(): lax.ppermute(value, 'row', [(s, s + steps) for s in range(count - steps)])  10.1 us
    ppermute x12, waiting for transfers between devices, around(): lax.ppermute(value, 'col', [(c, (c & 4) + (c + steps) % 4) for c in range...  8.64 us
    pallas_call x1, Pallas kernels, on_device(): call(functools.partial(near_far_kernel, 1), [shape(block_set, BF16)] * 4...  8.08 us
    ppermute x2, starting transfers between devices, passed_up(): lax.ppermute(value, 'row', [(s, s + steps) for s in range(count - steps)])  7.6 us
    ppermute x2, starting transfers between devices, across(): return lax.ppermute(value, 'col', [(c, c ^ 4) for c in range(8)])  7.09 us
    ppermute x2, starting transfers between devices, passed_down(): lax.ppermute(value, 'row', [(s, s - steps) for s in range(steps, count)])  7.06 us
  transfers between devices with their start and end apart: 18, of which 4 were waited for; matrix products, arithmetic and copies ran while one was open for 0% of the time, Pallas kernels for 18%

commit v1 on v0

--- a/solution.py
+++ b/solution.py
@@ -531,7 +531,6 @@
 
     other = across(packed)
     after = passed_down(packed, 1)
-    second = passed_down(packed, 2)
     rows_list, _ = lax.optimization_barrier((pair_rows.reshape(1, SLOTS), packed))
 
     inverse, codes, counts = call(
@@ -557,6 +556,8 @@
 
     near_rows = [packed] + [around(packed, k) for k in (1, 2, 3)]
 
+    codes, late = lax.optimization_barrier((codes, packed))
+    second = passed_down(late, 2)
     features, vectors = call(
         feature_kernel,
         (shape((COLS, BLK, BLK), BF16), shape((COLS, VECS, BLK), BF16)),

time: 95 us -> 98.4 us (1.036)
  the two profiles are of different devices: /device:TPU:49 before, /device:TPU:32 now
where the time goes in v1:
time: 98.4 us; the launch traced here: 98.8 us
  Pallas kernels  41.1 us (42%)
  starting transfers between devices  36.8 us (37%)
  waiting for transfers between devices  19.8 us (20%)
  between operations  1.07 us (1%)
    pallas_call x1, Pallas kernels, on_device(): call(functools.partial(near_far_kernel, 0), [shape(block_set, F32)] + [sh...  22.4 us
    ppermute x12, starting transfers between devices, around(): lax.ppermute(value, 'col', [(c, (c & 4) + (c + steps) % 4) for c in range...  18.2 us
    ppermute x2, waiting for transfers between devices, passed_up(): lax.ppermute(value, 'row', [(s, s + steps) for s in range(count - steps)])  8.52 us
    ppermute x2, starting transfers between devices, across(): return lax.ppermute(value, 'col', [(c, c ^ 4) for c in range(8)])  8.47 us
    pallas_call x1, Pallas kernels, on_device(): call(functools.partial(near_far_kernel, 1), [shape(block_set, BF16)] * 4...  6.92 us
    ppermute x2, waiting for transfers between devices, across(): return lax.ppermute(value, 'col', [(c, c ^ 4) for c in range(8)])  6.32 us
    ppermute x2, starting transfers between devices, passed_down(): lax.ppermute(value, 'row', [(s, s - steps) for s in range(steps, count)])  6.25 us
    ppermute x12, waiting for transfers between devices, around(): lax.ppermute(value, 'col', [(c, (c & 4) + (c + steps) % 4) for c in range...  4.94 us
  transfers between devices with their start and end apart: 18, of which 7 were waited for; matrix products, arithmetic and copies ran while one was open for 0% of the time, Pallas kernels for 25%

profile of v1, /device:TPU:32, one launch (start us, length us, event | category | flops | bytes accessed | tf_op | source)
XLA Modules:
  0.0 98.8 jit_solution(4122315120226879967)
XLA Ops:
  0.7 3.7 %prep.1.own.refs_2_ = bf16[32,24,128]{2,1,0:T(8,128)(2,1)} custom-call(f32[3,4096]{1,0:T(4,128)} %positions_hbm.1, s32[1,4096]{1,0:T(1,128)} %bitcast.4, f32[16,4096]{1,0:T(8,128)} %refs_9_.3, s32[32,128]{1,0:T(8,128)} %bitcast.6), custom_call_target="tpu_custom_call" | custom-call | tf_op jit(solution)/shard_map/prep/pallas_call | solution.py:515
  4.4 2.5 %side.1 = (s32[32,128]{1,0:T(8,128)}, s32[1,1280]{1,0:T(1,128)}, s32[2]{0:T(128)}) custom-call(s32[1,1]{1,0:T(1,128)S(6)} %copy.12.count_hbm, s32[1,512]{1,0:T(1,128)} %bitcast.8, s32[1,512]{1,0:T(1,128)} %bitcast.9, s32[32,128]{1,0:T(8,128)} %bitcast.7), custom_call_target="tpu_custom_call" | custom-call | flops 2000000000 | bytes 1000000 | tf_op jit(solution)/shard_map/side/pallas_call | solution.py:536
  6.9 4.3 %collective-permute-start.5 = (bf16[32,24,128]{2,1,0:T(8,128)(2,1)S(1)}, bf16[32,24,128]{2,1,0:T(8,128)(2,1)S(1)}, u32[]{:S(2)}, u32[]{:S(2)}) collective-permute-start(bf16[32,24,128]{2,1,0:T(8,128)(2,1)S(1)} %copy-done.1), channel_id=1, source_target_pairs={{16,0},{24,8},{32,16},{40,24},{48,32},{56,40},{64,48},{72,56},{80,... | collective-permute-start | bytes 589832 | tf_op jit(solution)/shard_map/ppermute | solution.py:493
  11.2 7.3 %collective-permute-start = (bf16[32,24,128]{2,1,0:T(8,128)(2,1)S(1)}, bf16[32,24,128]{2,1,0:T(8,128)(2,1)S(1)}, u32[]{:S(2)}, u32[]{:S(2)}) collective-permute-start(bf16[32,24,128]{2,1,0:T(8,128)(2,1)S(1)} %copy-done.1), channel_id=1, source_target_pairs={{0,4},{1,5},{2,6},{3,7},{4,0},{5,1},{6,2},{7,3},{8,12},{9,13},{10,... | collective-permute-start | bytes 589832 | tf_op jit(solution)/shard_map/ppermute | solution.py:502
  18.5 1.9 %collective-permute-start.4 = (bf16[32,24,128]{2,1,0:T(8,128)(2,1)S(1)}, bf16[32,24,128]{2,1,0:T(8,128)(2,1)S(1)}, u32[]{:S(2)}, u32[]{:S(2)}) collective-permute-start(bf16[32,24,128]{2,1,0:T(8,128)(2,1)S(1)} %copy-done.1), channel_id=1, source_target_pairs={{8,0},{16,8},{24,16},{32,24},{40,32},{48,40},{56,48},{64,56},{72,6... | collective-permute-start | bytes 589832 | tf_op jit(solution)/shard_map/ppermute | solution.py:493
  20.4 3.1 %collective-permute-start.8 = (bf16[32,24,128]{2,1,0:T(8,128)(2,1)S(1)}, bf16[32,24,128]{2,1,0:T(8,128)(2,1)S(1)}, u32[]{:S(2)}, u32[]{:S(2)}) collective-permute-start(bf16[32,24,128]{2,1,0:T(8,128)(2,1)S(1)} %copy-done.1), channel_id=1, source_target_pairs={{0,3},{1,0},{2,1},{3,2},{4,7},{5,4},{6,5},{7,6},{8,11},{9,8},{10,9... | collective-permute-start | bytes 589832 | tf_op jit(solution)/shard_map/ppermute | solution.py:506
  23.5 0.6 collective-permute-start.7
  24.2 1.0 collective-permute-start.6
  25.1 6.3 %collective-permute-done.refs_2_ = bf16[32,24,128]{2,1,0:T(8,128)(2,1)S(1)} collective-permute-done((bf16[32,24,128]{2,1,0:T(8,128)(2,1)S(1)}, bf16[32,24,128]{2,1,0:T(8,128)(2,1)S(1)}, u32[]{:S(2)}, u32[]{:S(2)}) %collective-permute-start) | collective-permute-done | bytes 196640 | tf_op jit(solution)/shard_map/ppermute | solution.py:502
  31.4 3.0 %collective-permute-start.3 = (bf16[32,24,128]{2,1,0:T(8,128)(2,1)S(1)}, bf16[32,24,128]{2,1,0:T(8,128)(2,1)S(1)}, u32[]{:S(2)}, u32[]{:S(2)}) collective-permute-start(bf16[32,24,128]{2,1,0:T(8,128)(2,1)S(1)} %collective-permute-done.refs_2_), channel_id=1, source_target_pairs={{0,3},{1,0},{2,1},{3,2},{4,7},{5,4},{6,5},{7,6},{8,11},{9,8},{10,9... | collective-permute-start | bytes 589832 | tf_op jit(solution)/shard_map/ppermute | solution.py:506
  34.5 0.6 collective-permute-start.2
  35.1 1.9 %features.1 = (bf16[96,128,128]{2,1,0:T(8,128)(2,1)S(1)}, bf16[96,16,128]{2,1,0:T(8,128)(2,1)S(1)}) custom-call(f32[6]{0:T(128)S(1)} %copy-done.5, bf16[32,24,128]{2,1,0:T(8,128)(2,1)S(1)} %copy-done.1, bf16[32,24,128]{2,1,0:T(8,128)(2,1)S(1)} %collective-permute-done.4.after, bf16[32,24,128]{2,1,0:T(8,128)(2,1)S(1)} %collective-permute-done.5.second), custom_call_target="tpu_custom_call" | custom-call | flops 12000000000 | bytes 1000000 | tf_op jit(solution)/shard_map/features/pallas_call | solution.py:561
  37.0 1.0 %collective-permute-start.1 = (bf16[32,24,128]{2,1,0:T(8,128)(2,1)S(1)}, bf16[32,24,128]{2,1,0:T(8,128)(2,1)S(1)}, u32[]{:S(2)}, u32[]{:S(2)}) collective-permute-start(bf16[32,24,128]{2,1,0:T(8,128)(2,1)S(1)} %collective-permute-done.refs_2_), channel_id=1, source_target_pairs={{0,1},{1,2},{2,3},{3,0},{4,5},{5,6},{6,7},{7,4},{8,9},{9,10},{10,1... | collective-permute-start | bytes 589832 | tf_op jit(solution)/shard_map/ppermute | solution.py:506
  38.1 22.4 %pairs_near.1 = (f32[32,16,128]{2,1,0:T(8,128)S(1)}, bf16[32,16,128]{2,1,0:T(8,128)(2,1)S(1)}, bf16[32,16,128]{2,1,0:T(8,128)(2,1)S(1)}, bf16[32,16,128]{2,1,0:T(8,128)(2,1)S(1)}, f32[96,16,128]{2,1,0:T(8,128)S(1)}) custom-call(s32[2]{0:T(128)S(1)} %copy-done.9, s32[1,1280]{1,0:T(1,128)S(1)} %copy-done.8, bf16[32,24,128]{2,1,0:T(8,128)(2,1)S(1)} %copy-done.1, ...), custom_call_target="tpu_custom_call" | custom-call | flops 16000000000 | bytes 1000000 | tf_op jit(solution)/shard_map/pairs_near/pallas_call | solution.py:582
  60.6 6.9 %pairs_far.1 = (bf16[32,16,128]{2,1,0:T(8,128)(2,1)S(1)}, bf16[32,16,128]{2,1,0:T(8,128)(2,1)S(1)}, bf16[32,16,128]{2,1,0:T(8,128)(2,1)S(1)}, bf16[32,16,128]{2,...) custom-call(s32[2]{0:T(128)S(1)} %copy-done.9, ...), custom_call_target="tpu_custom_call" | custom-call | flops 16000000000 | bytes 1000000 | tf_op jit(solution)/shard_map/pairs_far/pallas_call | solution.py:592
  67.5 0.1 collective-permute-start.9
  67.6 0.1 collective-permute-start.10
  67.7 3.1 %collective-permute-start.11 = (bf16[32,16,128]{2,1,0:T(8,128)(2,1)S(1)}, bf16[32,16,128]{2,1,0:T(8,128)(2,1)S(1)}, u32[]{:S(2)}, u32[]{:S(2)}) collective-permute-start(bf16[32,16,128]{2,1,0:T(8,128)(2,1)S(1)} %get-tuple-element.43), channel_id=1, source_target_pairs={{0,3},{1,0},{2,1},{3,2},{4,7},{5,4},{6,5},{7,6},{8,11},{9,8},{10,9... | collective-permute-start | bytes 393224 | tf_op jit(solution)/shard_map/ppermute | solution.py:506
  70.9 1.9 %collective-permute-start.13 = (bf16[32,16,128]{2,1,0:T(8,128)(2,1)S(1)}, bf16[32,16,128]{2,1,0:T(8,128)(2,1)S(1)}, u32[]{:S(2)}, u32[]{:S(2)}) collective-permute-start(bf16[32,16,128]{2,1,0:T(8,128)(2,1)S(1)} %get-tuple-element.44), channel_id=1, source_target_pairs={{0,8},{8,16},{16,24},{24,32},{32,40},{40,48},{48,56},{56,64},{64,7... | collective-permute-start | bytes 393224 | tf_op jit(solution)/shard_map/ppermute | solution.py:498
  72.8 1.9 %collective-permute-start.14 = (bf16[32,16,128]{2,1,0:T(8,128)(2,1)S(1)}, bf16[32,16,128]{2,1,0:T(8,128)(2,1)S(1)}, u32[]{:S(2)}, u32[]{:S(2)}) collective-permute-start(bf16[32,16,128]{2,1,0:T(8,128)(2,1)S(1)} %get-tuple-element.45), channel_id=1, source_target_pairs={{0,16},{8,24},{16,32},{24,40},{32,48},{40,56},{48,64},{56,72},{64,... | collective-permute-start | bytes 393224 | tf_op jit(solution)/shard_map/ppermute | solution.py:498
  74.7 0.5 collective-permute-done.9.refs_1_
  75.2 0.9 collective-permute-done.11.refs_3_
  76.1 0.1 far_sum.1
  76.2 1.2 %collective-permute-start.12 = (bf16[32,16,128]{2,1,0:T(8,128)(2,1)S(1)}, bf16[32,16,128]{2,1,0:T(8,128)(2,1)S(1)}, u32[]{:S(2)}, u32[]{:S(2)}) collective-permute-start(bf16[32,16,128]{2,1,0:T(8,128)(2,1)S(1)} %far_sum.1), channel_id=1, source_target_pairs={{0,4},{1,5},{2,6},{3,7},{4,0},{5,1},{6,2},{7,3},{8,12},{9,13},{10,... | collective-permute-start | bytes 393224 | tf_op jit(solution)/shard_map/ppermute | solution.py:502
  77.4 1.9 %collective-permute-done.13.refs_2_ = bf16[32,16,128]{2,1,0:T(8,128)(2,1)S(1)} collective-permute-done((bf16[32,16,128]{2,1,0:T(8,128)(2,1)S(1)}, bf16[32,16,128]{2,1,0:T(8,128)(2,1)S(1)}, u32[]{:S(2)}, u32[]{:S(2)}) %collective-permute-start.13) | collective-permute-done | bytes 131104 | tf_op jit(solution)/shard_map/ppermute | solution.py:498
  79.2 6.7 %collective-permute-done.14.refs_3_ = bf16[32,16,128]{2,1,0:T(8,128)(2,1)S(1)} collective-permute-done((bf16[32,16,128]{2,1,0:T(8,128)(2,1)S(1)}, bf16[32,16,128]{2,1,0:T(8,128)(2,1)S(1)}, u32[]{:S(2)}, u32[]{:S(2)}) %collective-permute-start.14) | collective-permute-done | bytes 131104 | tf_op jit(solution)/shard_map/ppermute | solution.py:498
  85.9 0.9 collective-permute-start.15
  86.8 2.1 %collective-permute-start.16 = (bf16[32,16,128]{2,1,0:T(8,128)(2,1)S(1)}, bf16[32,16,128]{2,1,0:T(8,128)(2,1)S(1)}, u32[]{:S(2)}, u32[]{:S(2)}) collective-permute-start(bf16[32,16,128]{2,1,0:T(8,128)(2,1)S(1)} %get-tuple-element.52), channel_id=1, source_target_pairs={{0,2},{1,3},{2,0},{3,1},{4,6},{5,7},{6,4},{7,5},{8,10},{9,11},{10,... | collective-permute-start | bytes 393224 | tf_op jit(solution)/shard_map/ppermute | solution.py:506
  88.8 2.6 %collective-permute-start.17 = (bf16[32,16,128]{2,1,0:T(8,128)(2,1)S(1)}, bf16[32,16,128]{2,1,0:T(8,128)(2,1)S(1)}, u32[]{:S(2)}, u32[]{:S(2)}) collective-permute-start(bf16[32,16,128]{2,1,0:T(8,128)(2,1)S(1)} %get-tuple-element.53), channel_id=1, source_target_pairs={{0,3},{1,0},{2,1},{3,2},{4,7},{5,4},{6,5},{7,6},{8,11},{9,8},{10,9... | collective-permute-start | bytes 393224 | tf_op jit(solution)/shard_map/ppermute | solution.py:506
  91.5 3.0 %collective-permute-done.15.refs_5_ = bf16[32,16,128]{2,1,0:T(8,128)(2,1)S(1)} collective-permute-done((bf16[32,16,128]{2,1,0:T(8,128)(2,1)S(1)}, bf16[32,16,128]{2,1,0:T(8,128)(2,1)S(1)}, u32[]{:S(2)}, u32[]{:S(2)}) %collective-permute-start.15) | collective-permute-done | bytes 131104 | tf_op jit(solution)/shard_map/ppermute | solution.py:506
  94.5 0.5 collective-permute-done.17.refs_7_
  95.0 3.7 %final.1 = f32[16,4096]{1,0:T(8,128)} custom-call(f32[6]{0:T(128)S(1)} %copy-done.4, f32[32,16,128]{2,1,0:T(8,128)S(1)} %get-tuple-element.39.refs_0_, bf16[32,16,128]{2,1,0:T(8,128)(2,1)S(1)} %collective-permute-done.12.refs_1_, bf16[32,16,128]{2,1,0:T(8,128)(2,1)S(1)} %collective-permute-done.13.refs_2_, ...), custom_call_target="tpu_custom_call" | custom-call | tf_op jit(solution)/shard_map/final/pallas_call | solution.py:613
  (31 shorter events, 0.1 us)
Async XLA Ops:
  4.3 2.5 %copy-start.1 = (bf16[32,24,128]{2,1,0:T(8,128)(2,1)S(1)}, bf16[32,24,128]{2,1,0:T(8,128)(2,1)}, u32[]{:S(2)}) copy-start(bf16[32,24,128]{2,1,0:T(8,128)(2,1)} %prep.1.own.refs_2_) | copy-start | bytes 589828
  4.3 30.8 %copy-start.5 = (f32[6]{0:T(128)S(1)}, f32[6]{0:T(128)}, u32[]{:S(2)}) copy-start(f32[6]{0:T(128)} %type_width.1) | copy-start | bytes 76
  6.8 31.2 %copy-start.6 = (bf16[135,16,128]{2,1,0:T(8,128)(2,1)S(1)}, bf16[135,16,128]{2,1,0:T(8,128)(2,1)}, u32[]{:S(2)}) copy-start(bf16[135,16,128]{2,1,0:T(8,128)(2,1)} %constant.5.clone.refs_9_) | copy-start | bytes 1658884
  6.9 31.2 %copy-start.7 = (bf16[135,16,128]{2,1,0:T(8,128)(2,1)S(1)}, bf16[135,16,128]{2,1,0:T(8,128)(2,1)}, u32[]{:S(2)}) copy-start(bf16[135,16,128]{2,1,0:T(8,128)(2,1)} %constant.4.clone.refs_8_) | copy-start | bytes 1658884
  6.9 31.2 %copy-start.8 = (s32[1,1280]{1,0:T(1,128)S(1)}, s32[1,1280]{1,0:T(1,128)}, u32[]{:S(2)}) copy-start(s32[1,1280]{1,0:T(1,128)} %get-tuple-element.34.refs_1_) | copy-start | bytes 15364
  6.9 31.2 %copy-start.9 = (s32[2]{0:T(128)S(1)}, s32[2]{0:T(128)}, u32[]{:S(2)}) copy-start(s32[2]{0:T(128)} %get-tuple-element.31.refs_0_) | copy-start | bytes 28
  6.9 17.3 %collective-permute-start.5 = (bf16[32,24,128]{2,1,0:T(8,128)(2,1)S(1)}, bf16[32,24,128]{2,1,0:T(8,128)(2,1)S(1)}, u32[]{:S(2)}, u32[]{:S(2)}) collective-permute-start(bf16[32,24,128]{2,1,0:T(8,128)(2,1)S(1)} %copy-done.1), channel_id=1, source_target_pairs={{16,0},{24,8},{32,16},{40,24},{48,32},{56,40},{64,48},{72,56},{80,... | collective-permute-start | bytes 589832 | tf_op jit(solution)/shard_map/ppermute | solution.py:493
  11.2 20.2 %collective-permute-start = (bf16[32,24,128]{2,1,0:T(8,128)(2,1)S(1)}, bf16[32,24,128]{2,1,0:T(8,128)(2,1)S(1)}, u32[]{:S(2)}, u32[]{:S(2)}) collective-permute-start(bf16[32,24,128]{2,1,0:T(8,128)(2,1)S(1)} %copy-done.1), channel_id=1, source_target_pairs={{0,4},{1,5},{2,6},{3,7},{4,0},{5,1},{6,2},{7,3},{8,12},{9,13},{10,... | collective-permute-start | bytes 589832 | tf_op jit(solution)/shard_map/ppermute | solution.py:502
  18.5 16.0 %collective-permute-start.4 = (bf16[32,24,128]{2,1,0:T(8,128)(2,1)S(1)}, bf16[32,24,128]{2,1,0:T(8,128)(2,1)S(1)}, u32[]{:S(2)}, u32[]{:S(2)}) collective-permute-start(bf16[32,24,128]{2,1,0:T(8,128)(2,1)S(1)} %copy-done.1), channel_id=1, source_target_pairs={{8,0},{16,8},{24,16},{32,24},{40,32},{48,40},{56,48},{64,56},{72,6... | collective-permute-start | bytes 589832 | tf_op jit(solution)/shard_map/ppermute | solution.py:493
  20.4 16.6 %collective-permute-start.8 = (bf16[32,24,128]{2,1,0:T(8,128)(2,1)S(1)}, bf16[32,24,128]{2,1,0:T(8,128)(2,1)S(1)}, u32[]{:S(2)}, u32[]{:S(2)}) collective-permute-start(bf16[32,24,128]{2,1,0:T(8,128)(2,1)S(1)} %copy-done.1), channel_id=1, source_target_pairs={{0,3},{1,0},{2,1},{3,2},{4,7},{5,4},{6,5},{7,6},{8,11},{9,8},{10,9... | collective-permute-start | bytes 589832 | tf_op jit(solution)/shard_map/ppermute | solution.py:506
  23.5 14.5 %collective-permute-start.7 = (bf16[32,24,128]{2,1,0:T(8,128)(2,1)S(1)}, bf16[32,24,128]{2,1,0:T(8,128)(2,1)S(1)}, u32[]{:S(2)}, u32[]{:S(2)}) collective-permute-start(bf16[32,24,128]{2,1,0:T(8,128)(2,1)S(1)} %copy-done.1), channel_id=1, source_target_pairs={{0,2},{1,3},{2,0},{3,1},{4,6},{5,7},{6,4},{7,5},{8,10},{9,11},{10,... | collective-permute-start | bytes 589832 | tf_op jit(solution)/shard_map/ppermute | solution.py:506
  24.2 13.9 %collective-permute-start.6 = (bf16[32,24,128]{2,1,0:T(8,128)(2,1)S(1)}, bf16[32,24,128]{2,1,0:T(8,128)(2,1)S(1)}, u32[]{:S(2)}, u32[]{:S(2)}) collective-permute-start(bf16[32,24,128]{2,1,0:T(8,128)(2,1)S(1)} %copy-done.1), channel_id=1, source_target_pairs={{0,1},{1,2},{2,3},{3,0},{4,5},{5,6},{6,7},{7,4},{8,9},{9,10},{10,1... | collective-permute-start | bytes 589832 | tf_op jit(solution)/shard_map/ppermute | solution.py:506
  31.4 29.1 %collective-permute-start.3 = (bf16[32,24,128]{2,1,0:T(8,128)(2,1)S(1)}, bf16[32,24,128]{2,1,0:T(8,128)(2,1)S(1)}, u32[]{:S(2)}, u32[]{:S(2)}) collective-permute-start(bf16[32,24,128]{2,1,0:T(8,128)(2,1)S(1)} %collective-permute-done.refs_2_), channel_id=1, source_target_pairs={{0,3},{1,0},{2,1},{3,2},{4,7},{5,4},{6,5},{7,6},{8,11},{9,8},{10,9... | collective-permute-start | bytes 589832 | tf_op jit(solution)/shard_map/ppermute | solution.py:506
  34.5 26.1 %collective-permute-start.2 = (bf16[32,24,128]{2,1,0:T(8,128)(2,1)S(1)}, bf16[32,24,128]{2,1,0:T(8,128)(2,1)S(1)}, u32[]{:S(2)}, u32[]{:S(2)}) collective-permute-start(bf16[32,24,128]{2,1,0:T(8,128)(2,1)S(1)} %collective-permute-done.refs_2_), channel_id=1, source_target_pairs={{0,2},{1,3},{2,0},{3,1},{4,6},{5,7},{6,4},{7,5},{8,10},{9,11},{10,... | collective-permute-start | bytes 589832 | tf_op jit(solution)/shard_map/ppermute | solution.py:506
  37.0 23.6 %collective-permute-start.1 = (bf16[32,24,128]{2,1,0:T(8,128)(2,1)S(1)}, bf16[32,24,128]{2,1,0:T(8,128)(2,1)S(1)}, u32[]{:S(2)}, u32[]{:S(2)}) collective-permute-start(bf16[32,24,128]{2,1,0:T(8,128)(2,1)S(1)} %collective-permute-done.refs_2_), channel_id=1, source_target_pairs={{0,1},{1,2},{2,3},{3,0},{4,5},{5,6},{6,7},{7,4},{8,9},{9,10},{10,1... | collective-permute-start | bytes 589832 | tf_op jit(solution)/shard_map/ppermute | solution.py:506
  60.6 34.4 %copy-start = (f32[16,4096]{1,0:T(8,128)S(1)}, f32[16,4096]{1,0:T(8,128)}, u32[]{:S(2)}) copy-start(f32[16,4096]{1,0:T(8,128)} %refs_9_.3) | copy-start | bytes 786436
  60.6 34.4 %copy-start.2 = (s32[4096]{0:T(1024)S(1)}, s32[4096]{0:T(1024)}, u32[]{:S(2)}) copy-start(s32[4096]{0:T(1024)} %param.12) | copy-start | bytes 49156
  60.6 34.4 %copy-start.3 = (s32[32,128]{1,0:T(8,128)S(1)}, s32[32,128]{1,0:T(8,128)}, u32[]{:S(2)}) copy-start(s32[32,128]{1,0:T(8,128)} %get-tuple-element.54.refs_10_) | copy-start | bytes 49156
  60.6 34.4 %copy-start.4 = (f32[6]{0:T(128)S(1)}, f32[6]{0:T(128)}, u32[]{:S(2)}) copy-start(f32[6]{0:T(128)} %type_hard.1) | copy-start | bytes 76
  67.5 7.7 %collective-permute-start.9 = (bf16[32,16,128]{2,1,0:T(8,128)(2,1)S(1)}, bf16[32,16,128]{2,1,0:T(8,128)(2,1)S(1)}, u32[]{:S(2)}, u32[]{:S(2)}) collective-permute-start(bf16[32,16,128]{2,1,0:T(8,128)(2,1)S(1)} %get-tuple-element.41), channel_id=1, source_target_pairs={{0,1},{1,2},{2,3},{3,0},{4,5},{5,6},{6,7},{7,4},{8,9},{9,10},{10,1... | collective-permute-start | bytes 393224 | tf_op jit(solution)/shard_map/ppermute | solution.py:506
  67.6 7.6 %collective-permute-start.10 = (bf16[32,16,128]{2,1,0:T(8,128)(2,1)S(1)}, bf16[32,16,128]{2,1,0:T(8,128)(2,1)S(1)}, u32[]{:S(2)}, u32[]{:S(2)}) collective-permute-start(bf16[32,16,128]{2,1,0:T(8,128)(2,1)S(1)} %get-tuple-element.42), channel_id=1, source_target_pairs={{0,2},{1,3},{2,0},{3,1},{4,6},{5,7},{6,4},{7,5},{8,10},{9,11},{10,... | collective-permute-start | bytes 393224 | tf_op jit(solution)/shard_map/ppermute | solution.py:506
  67.7 8.4 %collective-permute-start.11 = (bf16[32,16,128]{2,1,0:T(8,128)(2,1)S(1)}, bf16[32,16,128]{2,1,0:T(8,128)(2,1)S(1)}, u32[]{:S(2)}, u32[]{:S(2)}) collective-permute-start(bf16[32,16,128]{2,1,0:T(8,128)(2,1)S(1)} %get-tuple-element.43), channel_id=1, source_target_pairs={{0,3},{1,0},{2,1},{3,2},{4,7},{5,4},{6,5},{7,6},{8,11},{9,8},{10,9... | collective-permute-start | bytes 393224 | tf_op jit(solution)/shard_map/ppermute | solution.py:506
  70.9 8.4 %collective-permute-start.13 = (bf16[32,16,128]{2,1,0:T(8,128)(2,1)S(1)}, bf16[32,16,128]{2,1,0:T(8,128)(2,1)S(1)}, u32[]{:S(2)}, u32[]{:S(2)}) collective-permute-start(bf16[32,16,128]{2,1,0:T(8,128)(2,1)S(1)} %get-tuple-element.44), channel_id=1, source_target_pairs={{0,8},{8,16},{16,24},{24,32},{32,40},{40,48},{48,56},{56,64},{64,7... | collective-permute-start | bytes 393224 | tf_op jit(solution)/shard_map/ppermute | solution.py:498
  72.8 13.1 %collective-permute-start.14 = (bf16[32,16,128]{2,1,0:T(8,128)(2,1)S(1)}, bf16[32,16,128]{2,1,0:T(8,128)(2,1)S(1)}, u32[]{:S(2)}, u32[]{:S(2)}) collective-permute-start(bf16[32,16,128]{2,1,0:T(8,128)(2,1)S(1)} %get-tuple-element.45), channel_id=1, source_target_pairs={{0,16},{8,24},{16,32},{24,40},{32,48},{40,56},{48,64},{56,72},{64,... | collective-permute-start | bytes 393224 | tf_op jit(solution)/shard_map/ppermute | solution.py:498
  76.2 15.3 %collective-permute-start.12 = (bf16[32,16,128]{2,1,0:T(8,128)(2,1)S(1)}, bf16[32,16,128]{2,1,0:T(8,128)(2,1)S(1)}, u32[]{:S(2)}, u32[]{:S(2)}) collective-permute-start(bf16[32,16,128]{2,1,0:T(8,128)(2,1)S(1)} %far_sum.1), channel_id=1, source_target_pairs={{0,4},{1,5},{2,6},{3,7},{4,0},{5,1},{6,2},{7,3},{8,12},{9,13},{10,... | collective-permute-start | bytes 393224 | tf_op jit(solution)/shard_map/ppermute | solution.py:502
  85.9 8.6 %collective-permute-start.15 = (bf16[32,16,128]{2,1,0:T(8,128)(2,1)S(1)}, bf16[32,16,128]{2,1,0:T(8,128)(2,1)S(1)}, u32[]{:S(2)}, u32[]{:S(2)}) collective-permute-start(bf16[32,16,128]{2,1,0:T(8,128)(2,1)S(1)} %get-tuple-element.51), channel_id=1, source_target_pairs={{0,1},{1,2},{2,3},{3,0},{4,5},{5,6},{6,7},{7,4},{8,9},{9,10},{10,1... | collective-permute-start | bytes 393224 | tf_op jit(solution)/shard_map/ppermute | solution.py:506
  86.8 7.7 %collective-permute-start.16 = (bf16[32,16,128]{2,1,0:T(8,128)(2,1)S(1)}, bf16[32,16,128]{2,1,0:T(8,128)(2,1)S(1)}, u32[]{:S(2)}, u32[]{:S(2)}) collective-permute-start(bf16[32,16,128]{2,1,0:T(8,128)(2,1)S(1)} %get-tuple-element.52), channel_id=1, source_target_pairs={{0,2},{1,3},{2,0},{3,1},{4,6},{5,7},{6,4},{7,5},{8,10},{9,11},{10,... | collective-permute-start | bytes 393224 | tf_op jit(solution)/shard_map/ppermute | solution.py:506
  88.8 6.2 %collective-permute-start.17 = (bf16[32,16,128]{2,1,0:T(8,128)(2,1)S(1)}, bf16[32,16,128]{2,1,0:T(8,128)(2,1)S(1)}, u32[]{:S(2)}, u32[]{:S(2)}) collective-permute-start(bf16[32,16,128]{2,1,0:T(8,128)(2,1)S(1)} %get-tuple-element.53), channel_id=1, source_target_pairs={{0,3},{1,0},{2,1},{3,2},{4,7},{5,4},{6,5},{7,6},{8,11},{9,8},{10,9... | collective-permute-start | bytes 393224 | tf_op jit(solution)/shard_map/ppermute | solution.py:506
